TPU v7x, 512 devices: a whole 4x8x8 slice. The times are simulated.
512 devices in a mesh: cfg: 2 (over core), seq: 64 (over x, z, y_hi), tp: 4 (over y_lo).
Axes of the slice: x: 4, y: 8 (y_hi: 2, y_lo: 4; y = y_hi * 4 + y_lo), z: 8, core: 2. Of those that a mesh axis runs over, the one named last changes fastest.
Arguments:
- stream: bfloat16 [2, 2560, 3072], P('cfg', 'seq', 'tp'), may hold values from -6 to 6
- queries: bfloat16 [2, 2560, 1536], P('cfg', 'seq', 'tp'), may hold values from -6 to 6
- keys: bfloat16 [2, 2560, 1536], P('cfg', 'seq', 'tp'), may hold values from -6 to 6
- values: bfloat16 [2, 2560, 1536], P('cfg', 'seq', 'tp'), may hold values from -6 to 6
- text_keys: bfloat16 [2, 226, 1536], P('cfg', None, 'tp'), may hold values from -6 to 6
- text_values: bfloat16 [2, 226, 1536], P('cfg', None, 'tp'), may hold values from -6 to 6
- out_weight: bfloat16 [1536, 3072], P('tp'), may hold values from -0.15625 to 0.15625
- gate: float32 [3072], P('tp'), may hold values from -4 to 4
- shift: float32 [3072], P('tp'), may hold values from -3 to 3
- scale: float32 [3072], P('tp'), may hold values from -3 to 3
- proj_weight: float32 [3072, 64], P('tp'), may hold values from -0.109375 to 0.109375
- q_gain: float32 [64], replicated, may hold values from 1.4 to 6
- k_gain: float32 [64], replicated, may hold values from 1.4 to 6
- lengths: int32 [64], replicated, may hold values from 1 to 40, 2304 in all
- latents: float32 [2560, 64], P('seq', ('cfg', 'tp')), may hold values from -6 to 6
- alphas: float32 [1000], replicated, may hold values from 0.05 to 0.95
- step_index: int32 [1], replicated, may hold values from 20 to 999
Outputs:
- hidden_out: bfloat16 [2, 2560, 3072], P('cfg', 'seq', 'tp')
- latents_out: float32 [2560, 64], P('seq', ('cfg', 'tp'))
Inputs may be any that keep to these rules, and one draw needn't show every extreme that they name: `lengths`: video tokens held by each index of seq, in token order; they sum to 2304 and the largest is exactly 40. The previous step's entry is step_index - 20.
All inputs are finite; a program needn't handle non-finite values.
Results may differ from a plain program's by a relative error of at most 0.012.
The roundings to bfloat16 on the way count: a program that leaves them out, or rounds other values in their place, can miss the bound.
Values may be sent and summed in bfloat16 or wider, within the bound.
A program may use at most 64 MiB of HBM per device.

v0:
```python
import jax
import jax.numpy as jnp
from jax import lax
from jax.sharding import PartitionSpec as P

D = 3072
HEAD = 64
HP = 30
WP = 45
STRIDE = 20
guide_scale = 6.0
head_eps = 1e-06
final_eps = 1e-05


def partner_2(shard, axis, distance):
    return lax.ppermute(shard, axis, [(i, i ^ 1 << distance) for i in range(lax.axis_size(axis))])


def rope_tables(position):
    frame = position // (HP * WP)
    height = position // WP % HP
    across = position % WP

    def angles(coord, extent):
        freq = 1.0 / 10000.0 ** (jnp.arange(0, extent, 2, dtype=jnp.float32) / extent)
        return coord.astype(jnp.float32)[:, None] * freq[None, :]

    angle = jnp.concatenate([angles(frame, 16), angles(height, 24), angles(across, 24)], axis=1)
    return (jnp.cos(angle), jnp.sin(angle))


def head_norm(field, gain):
    centre = field - jnp.mean(field, axis=-1, keepdims=True)
    spread = jnp.mean(centre * centre, axis=-1, keepdims=True)
    return centre * lax.rsqrt(spread + head_eps) * gain


def rotate_pairs(field, cos_table, sin_table):
    pairs = field.reshape(field.shape[:-1] + (HEAD // 2, 2))
    first = pairs[..., 0]
    second = pairs[..., 1]
    cos_part = cos_table[:, None, :]
    sin_part = sin_table[:, None, :]
    turned = jnp.stack(
        [first * cos_part - second * sin_part, second * cos_part + first * sin_part], axis=-1
    )
    return turned.reshape(field.shape)


def prepare(field, gain, tables):
    count = field.shape[0]
    normed = head_norm(field.astype(jnp.float32).reshape(count, -1, HEAD), gain)
    if tables is not None:
        normed = rotate_pairs(normed, tables[0], tables[1])
    return normed.reshape(count, -1).astype(jnp.bfloat16)


def last_dims(left, right):
    return lax.dot_general(
        left, right, (((1,), (1,)), ((), ())), preferred_element_type=jnp.float32
    )


def shards(
    stream,
    queries,
    keys,
    values,
    text_keys,
    text_values,
    out_weight,
    gate,
    shift,
    scale,
    proj_weight,
    q_gain,
    k_gain,
    lengths,
    latents,
    alphas,
    step_index,
):
    blocks = lax.axis_size("seq")
    group = lax.axis_size("tp")
    rows = queries.shape[1]
    width = queries.shape[2]
    heads_here = width // HEAD
    seq_rank = lax.axis_index("seq")
    order = jnp.arange(blocks, dtype=jnp.int32)
    own_start = jnp.sum(jnp.where(order < seq_rank, lengths, 0))
    own_count = jnp.sum(jnp.where(order == seq_rank, lengths, 0))
    within = jnp.arange(rows, dtype=jnp.int32)
    own_live = within < own_count
    own_tables = rope_tables(own_start + within)
    query_hat = prepare(queries[0], q_gain, own_tables)
    outgoing = keys[0]
    arrived_keys, arrived_values = (
        lax.all_gather(outgoing, "seq", axis=0, tiled=True),
        lax.all_gather(values[0], "seq", axis=0, tiled=True),
    )
    offsets = jnp.cumsum(lengths) - lengths
    all_positions = (offsets[:, None] + within[None, :]).reshape(-1)
    video_keys = prepare(arrived_keys, k_gain, rope_tables(all_positions))
    video_live = (within[None, :] < lengths[:, None]).reshape(-1)
    text_hat = prepare(text_keys[0], k_gain, None)
    text_vals = text_values[0]

    def one_head(head):
        start = head * HEAD
        query_part = lax.dynamic_slice_in_dim(query_hat, start, HEAD, 1)
        video_key_part = lax.dynamic_slice_in_dim(video_keys, start, HEAD, 1)
        video_value_part = lax.dynamic_slice_in_dim(arrived_values, start, HEAD, 1)
        text_key_part = lax.dynamic_slice_in_dim(text_hat, start, HEAD, 1)
        text_value_part = lax.dynamic_slice_in_dim(text_vals, start, HEAD, 1)
        video_scores = last_dims(query_part, video_key_part) * 0.125
        video_scores = jnp.where(video_live[None, :], video_scores, -jnp.inf)
        text_scores = last_dims(query_part, text_key_part) * 0.125
        row_max = jnp.maximum(
            jnp.max(video_scores, axis=1, keepdims=True),
            jnp.max(text_scores, axis=1, keepdims=True),
        )
        video_weights = jnp.exp(video_scores - row_max)
        text_weights = jnp.exp(text_scores - row_max)
        totals = jnp.sum(video_weights, axis=1, keepdims=True) + jnp.sum(
            text_weights, axis=1, keepdims=True
        )
        mixed = jnp.dot(
            video_weights.astype(jnp.bfloat16), video_value_part, preferred_element_type=jnp.float32
        )
        mixed = mixed + jnp.dot(
            text_weights.astype(jnp.bfloat16), text_value_part, preferred_element_type=jnp.float32
        )
        return (mixed / totals).astype(jnp.bfloat16)

    attended = lax.map(one_head, jnp.arange(heads_here, dtype=jnp.int32))
    attended = jnp.transpose(attended, (1, 0, 2)).reshape(rows, width)
    projected = jnp.dot(attended, out_weight, preferred_element_type=jnp.float32)
    summed = lax.psum_scatter(
        projected.astype(jnp.bfloat16), "tp", scatter_dimension=1, tiled=True
    ).astype(jnp.float32)
    hidden = stream[0].astype(jnp.float32) + gate * summed
    hidden = jnp.where(own_live[:, None], hidden, 0.0).astype(jnp.bfloat16)
    widened = lax.optimization_barrier(hidden).astype(jnp.float32)
    row_total, row_square = lax.psum(
        (jnp.sum(widened, axis=1), jnp.sum(widened * widened, axis=1)), "tp"
    )
    mean = row_total[:, None] / D
    square = row_square[:, None] / D
    normed = (widened - mean) * lax.rsqrt(square - mean * mean + final_eps) * (1.0 + scale) + shift
    partial_pred = jnp.dot(
        normed, proj_weight, precision=lax.Precision.HIGHEST, preferred_element_type=jnp.float32
    )
    cfg_rank = lax.axis_index("cfg")
    tp_rank = lax.axis_index("tp")
    piece = proj_weight.shape[1] // (2 * group)
    prediction = lax.psum(partial_pred, "tp")
    partner = partner_2(prediction, "cfg", 0)
    column = (cfg_rank * group + tp_rank) * piece
    mine = lax.dynamic_slice_in_dim(prediction, column, piece, 1)
    theirs = lax.dynamic_slice_in_dim(partner, column, piece, 1)
    is_conditioned = cfg_rank == 0
    conditioned = jnp.where(is_conditioned, mine, theirs)
    unconditioned = jnp.where(is_conditioned, theirs, mine)
    guided = unconditioned + guide_scale * (conditioned - unconditioned)
    current = alphas[step_index[0]]
    earlier = alphas[step_index[0] - STRIDE]
    root_now = jnp.sqrt(current)
    rest_now = jnp.sqrt(1.0 - current)
    clean = root_now * latents - rest_now * guided
    noise = root_now * guided + rest_now * latents
    stepped = jnp.sqrt(earlier) * clean + jnp.sqrt(1.0 - earlier) * noise
    latents_out = jnp.where(own_live[:, None], stepped, 0.0)
    return (hidden[None], latents_out)


def solution(mesh):
    return jax.shard_map(
        shards,
        mesh=mesh,
        in_specs=(
            P("cfg", "seq", "tp"),
            P("cfg", "seq", "tp"),
            P("cfg", "seq", "tp"),
            P("cfg", "seq", "tp"),
            P("cfg", None, "tp"),
            P("cfg", None, "tp"),
            P("tp", None),
            P("tp"),
            P("tp"),
            P("tp"),
            P("tp", None),
            P(),
            P(),
            P(),
            P("seq", ("cfg", "tp")),
            P(),
            P(),
        ),
        out_specs=(P("cfg", "seq", "tp"), P("seq", ("cfg", "tp"))),
        check_vma=False,
    )
```

profile of v0, /device:TPU:1, one launch (start us, length us, event | category | flops | bytes accessed | tf_op | source)
XLA Modules:
  0.0 389.1 jit_solution(11699721490610072539)
XLA Ops:
  7.2 0.7 all-gather.5.cloned.1.call-update
  8.0 0.7 all-gather.7.cloned.1.call-update
  8.7 0.7 copy.55
  9.7 1.3 fusion.51
  11.2 0.7 fusion.53
  11.9 0.7 fusion.57
  12.6 0.9 reshape.432
  13.4 0.9 copy.50
  14.8 0.8 mul.360
  16.3 0.8 mul.340
  18.6 1.4 fusion.29
  20.0 127.2 %all-gather.5.cloned.1.call-done = bf16[1,2560,384]{2,1,0:T(8,128)(2,1)} async-done(((bf16[1,40,384]{2,1,0:T(8,128)(2,1)}), bf16[1,2560,384]{2,1,0:T(8,128)(2,1)}) %all-gather.5.cloned.1.call-update) | async-done | bytes 1966096 | tf_op jit(solution)/shard_map/all_gather | solution.py:99
  147.2 4.0 %copy.54 = bf16[1,2560,384]{1,2,0:T(8,128)(2,1)} copy(bf16[1,2560,384]{2,1,0:T(8,128)(2,1)} %all-gather.5.cloned.1.call-done) | data formatting | bytes 3932160 | tf_op jit(solution)/shard_map/all_gather | solution.py:99
  151.2 3.9 %convert_element_type.154 = f32[1,2560,384]{1,2,0:T(8,128)} convert(bf16[1,2560,384]{1,2,0:T(8,128)(2,1)} %copy.54) | non-fusion elementwise | flops 983040 | bytes 5898240 | tf_op jit(solution)/shard_map/convert_element_type | solution.py:53
  155.1 2.5 reduce_sum.112
  157.6 5.3 %reshape.425 = f32[2560,6,32,2]{0,3,2,1:T(2,128)} reshape(bf16[1,2560,384]{1,2,0:T(8,128)(2,1)} %copy.54) | data formatting | bytes 5898240 | tf_op jit(solution)/shard_map/reshape | solution.py:53
  162.9 2.8 multiply_reduce_fusion
  166.2 1.8 multiply_multiply_fusion
  168.0 5.2 %subtract_convert_fusion = (bf16[2560,6,32,1]{0,3,2,1:T(2,128)(2,1)S(1)}, bf16[2560,6,32,1]{0,3,2,1:T(2,128)(2,1)S(1)}) fusion(f32[2560,6,32,2]{0,3,2,1:T(2,128)S(1)} %multiply_multiply_fusion, f32[2560,32]{0,1:T(8,128)S(1)} %get-tuple-element.135, f32[2560,32]{0,1:T(8,128)S(1)} %get-tuple-element.134), kind=kLoop, calls=%fused_computation.34 | loop fusion | flops 3932160 | bytes 6553600 | tf_op jit(solution)/shard_map/convert.5
  173.2 5.7 %pad_maximum_fusion = bf16[2560,6,32,2]{0,3,2,1:T(2,128)(2,1)} fusion(bf16[2560,6,32,1]{0,3,2,1:T(2,128)(2,1)S(1)} %get-tuple-element.133, bf16[2560,6,32,1]{0,3,2,1:T(2,128)(2,1)S(1)} %get-tuple-element.132), kind=kLoop, calls=%fused_computation.32 | loop fusion | flops 3932160 | bytes 3932160 | tf_op jit(solution)/shard_map/stack | solution.py:45
  178.9 5.2 %convert_element_type.139 = bf16[2560,384]{0,1:T(8,128)(2,1)} reshape(bf16[2560,6,32,2]{0,3,2,1:T(2,128)(2,1)} %pad_maximum_fusion) | data formatting | bytes 3932160 | tf_op jit(solution)/shard_map/convert_element_type | solution.py:56
  184.1 96.8 %all-gather.7.cloned.1.call-done = bf16[1,2560,384]{2,1,0:T(8,128)(2,1)} async-done(((bf16[1,40,384]{2,1,0:T(8,128)(2,1)}), bf16[1,2560,384]{2,1,0:T(8,128)(2,1)}) %all-gather.7.cloned.1.call-update) | async-done | bytes 1966096 | tf_op jit(solution)/shard_map/all_gather | solution.py:100
  281.0 36.7 %while.11 = (s32[]{:T(128)}, bf16[6,40,64]{2,1,0:T(8,128)(2,1)S(1)}, s32[6]{0:T(128)S(1)}, bf16[40,384]{1,0:T(8,128)(2,1)S(1)}, bf16[2560,384]{0,1:T(8,128)(2,1)...) while((s32[]{:T(128)}, ...), condition=%wide.region_14.15_spmd.clone, body=%wide.region_9.14_spmd.clone.sunk | while | flops 29309844 | bytes 2495583 | solution.py:136
  282.4 1.3 fusion.78
  284.5 1.5 fusion.80
  286.0 1.1 fusion.83
  288.5 1.3 fusion.78
  290.6 1.5 fusion.80
  292.1 1.1 fusion.83
  294.6 1.3 fusion.78
  296.8 1.5 fusion.80
  298.2 1.1 fusion.83
  300.8 1.3 fusion.78
  302.9 1.5 fusion.80
  304.4 1.1 fusion.83
  306.9 1.3 fusion.78
  309.0 1.5 fusion.80
  310.5 1.1 fusion.83
  313.0 1.3 fusion.78
  315.1 1.5 fusion.80
  316.6 1.1 fusion.83
  317.9 1.2 convolution_convert_fusion
  319.8 24.9 %reduce-scatter.2.cloned.1.call-done = bf16[40,768]{1,0:T(8,128)(2,1)} async-done(((bf16[40,3072]{1,0:T(8,128)(2,1)}), bf16[40,768]{1,0:T(8,128)(2,1)}) %reduce-scatter.2.cloned.1.call-update) | async-done | bytes 61456 | tf_op jit(solution)/shard_map/reduce_scatter | solution.py:139
  344.8 0.9 fusion.37
  345.8 7.4 %all-reduce = (f32[40]{0:T(128)S(1)}, f32[40]{0:T(128)S(1)}) all-reduce(f32[40]{0:T(128)S(1)} %get-tuple-element.105, f32[40]{0:T(128)S(1)} %get-tuple-element.104), channel_id=1, replica_groups=mesh['cfg'=2,'seq'=64,'tp'=4] {'tp'}, use_global_device_ids=true, to_apply=%region_19.20 | all-reduce | flops 80 | bytes 640 | tf_op jit(solution)/shard_map/psum | solution.py:145
  353.6 13.4 %psum.23 = f32[40,64]{0,1:T(8,128)S(1)} all-reduce(f32[40,64]{0,1:T(8,128)S(1)} %fusion.33), channel_id=1, replica_groups=mesh['cfg'=2,'seq'=64,'tp'=4] {'tp'}, use_global_device_ids=true, to_apply=%region_20.21 | all-reduce | flops 2560 | bytes 20480 | tf_op jit(solution)/shard_map/psum | solution.py:157
  367.0 10.4 %collective-permute-start = (f32[40,64]{0,1:T(8,128)S(1)}, f32[40,64]{0,1:T(8,128)S(1)}, u32[]{:S(2)}, u32[]{:S(2)}) collective-permute-start(f32[40,64]{0,1:T(8,128)S(1)} %psum.23), channel_id=1, source_target_pairs={{0,256},{256,0},{1,257},{257,1},{2,258},{258,2},{3,259},{259,3},{4... | collective-permute-start | bytes 30728 | tf_op jit(solution)/shard_map/ppermute | solution.py:17
  378.0 1.4 fusion.60
  (125 shorter events, 14.9 us)
Async XLA Ops:
  7.2 310.8 %copy-start = (bf16[384,3072]{1,0:T(8,128)(2,1)S(1)}, bf16[384,3072]{1,0:T(8,128)(2,1)}, u32[]{:S(2)}) copy-start(bf16[384,3072]{1,0:T(8,128)(2,1)} %param.25) | copy-start | bytes 7077892
  7.2 11.1 %copy-start.11 = (f32[64]{0:T(128)S(1)}, f32[64]{0:T(128)}, u32[]{:S(2)}) copy-start(f32[64]{0:T(128)} %param.31) | copy-start | bytes 772
  7.2 10.8 %copy-start.4 = (bf16[1,226,384]{2,1,0:T(8,128)(2,1)S(1)}, bf16[1,226,384]{2,1,0:T(8,128)(2,1)}, u32[]{:S(2)}) copy-start(bf16[1,226,384]{2,1,0:T(8,128)(2,1)} %param.23) | copy-start | bytes 520708
  7.2 140.0 %all-gather.5.cloned.1.call-start = ((), (), s32[]{:S(2)}) async-start(), calls=%async_computation.2 | async-start | bytes 1996800 | tf_op jit(solution)/shard_map/all_gather | solution.py:99
  7.9 273.0 %all-gather.7.cloned.1.call-start = ((), (), s32[]{:S(2)}) async-start(), calls=%async_computation.3 | async-start | bytes 1996800 | tf_op jit(solution)/shard_map/all_gather | solution.py:100
  8.7 336.1 %reduce-scatter.2.cloned.1.call-start = ((), (), s32[]{:S(2)}) async-start(), calls=%async_computation.1 | async-start | bytes 307200 | tf_op jit(solution)/shard_map/reduce_scatter | solution.py:139
  162.9 3.3 copy-start.1
  178.9 102.1 %copy-start.6 = (s32[64]{0:T(128)S(1)}, s32[64]{0:T(128)}, u32[]{:S(2)}) copy-start(s32[64]{0:T(128)} %param.32) | copy-start | bytes 772
  317.7 2.1 copy-start.10
  317.7 27.1 %copy-start.5 = (bf16[1,40,768]{2,1,0:T(8,128)(2,1)S(1)}, bf16[1,40,768]{2,1,0:T(8,128)(2,1)}, u32[]{:S(2)}) copy-start(bf16[1,40,768]{2,1,0:T(8,128)(2,1)} %param.19) | copy-start | bytes 184324
  317.7 27.0 %copy-start.8 = (f32[768]{0:T(1024)S(1)}, f32[768]{0:T(1024)}, u32[]{:S(2)}) copy-start(f32[768]{0:T(1024)} %param.26) | copy-start | bytes 9220
  317.7 35.5 %copy-start.3 = (f32[768,64]{0,1:T(8,128)S(1)}, f32[768,64]{0,1:T(8,128)}, u32[]{:S(2)}) copy-start(f32[768,64]{0,1:T(8,128)} %param.29) | copy-start | bytes 589828
  317.7 35.5 %copy-start.7 = (f32[768]{0:T(1024)S(1)}, f32[768]{0:T(1024)}, u32[]{:S(2)}) copy-start(f32[768]{0:T(1024)} %param.27) | copy-start | bytes 9220
  317.8 64.2 %copy-start.9 = (f32[40,8]{0,1:T(8,128)S(1)}, f32[40,8]{0,1:T(8,128)}, u32[]{:S(2)}) copy-start(f32[40,8]{0,1:T(8,128)} %param.33) | copy-start | bytes 3844
  345.7 36.9 %copy-start.2 = (bf16[40,768]{1,0:T(8,128)(2,1)}, bf16[40,768]{1,0:T(8,128)(2,1)S(1)}, u32[]{:S(2)}) copy-start(bf16[40,768]{1,0:T(8,128)(2,1)S(1)} %fusion.37) | copy-start | bytes 184324
  367.0 15.0 %collective-permute-start = (f32[40,64]{0,1:T(8,128)S(1)}, f32[40,64]{0,1:T(8,128)S(1)}, u32[]{:S(2)}, u32[]{:S(2)}) collective-permute-start(f32[40,64]{0,1:T(8,128)S(1)} %psum.23), channel_id=1, source_target_pairs={{0,256},{256,0},{1,257},{257,1},{2,258},{258,2},{3,259},{259,3},{4... | collective-permute-start | bytes 30728 | tf_op jit(solution)/shard_map/ppermute | solution.py:17
Sparse Core Ops, SparseCore 0:
  12.4 134.7 all-gather.4
  151.5 129.3 all-gather.6
  319.3 25.4 reduce-scatter.1
where the time goes:
time: 391 us; the launch traced here: 389 us
  waiting for transfers between devices  250 us (64%)
  other arithmetic  33.5 us (9%)
  matrix products  26.8 us (7%)
  local copies, waits for them, and re-layouts  25.8 us (7%)
  blocking collectives  20.8 us (5%)
  between operations  17.4 us (4%)
  starting transfers between devices  10.5 us (3%)
  loops' own time  4.14 us (1%)
    all_gather x1, waiting for transfers between devices, shards(): lax.all_gather(outgoing, 'seq', axis=0, tiled=True)  127 us
    all_gather x1, waiting for transfers between devices, shards(): lax.all_gather(values[0], 'seq', axis=0, tiled=True)  96.8 us
    reduce_scatter x1, waiting for transfers between devices, shards(): lax.psum_scatter(projected.astype(jnp.bfloat16), 'tp', scatter_dimension=...  24.9 us
    psum x1, blocking collectives, shards(): prediction = lax.psum(partial_pred, 'tp')  13.4 us
    ppermute x1, starting transfers between devices, partner_2(): lax.ppermute(shard, axis, [(i, i ^ 1 << distance) for i in range(lax.axis...  10.4 us
    dot_general x12, matrix products, last_dims(): lax.dot_general(left, right, (((1,), (1,)), ((), ())), preferred_element_...  9.89 us
    dot_general x6, matrix products, one_head(): jnp.dot(video_weights.astype(jnp.bfloat16), video_value_part, preferred_e...  8.91 us
  transfers between devices with their start and end apart: 4, of which 3 were waited for; matrix products, arithmetic and copies ran while one was open for 13% of the time, Pallas kernels for 0%

commit v1 on v0

--- a/solution.py
+++ b/solution.py
@@ -97,7 +97,15 @@
     outgoing = keys[0]
     arrived_keys, arrived_values = (
         lax.all_gather(outgoing, "seq", axis=0, tiled=True),
-        lax.all_gather(values[0], "seq", axis=0, tiled=True),
+        jnp.concatenate(
+            lax.all_to_all(
+                jnp.stack(lax.axis_size("seq") * [values[0]], axis=0),
+                split_axis=0,
+                concat_axis=0,
+                axis_name="seq",
+            ),
+            axis=0,
+        ),
     )
     offsets = jnp.cumsum(lengths) - lengths
     all_positions = (offsets[:, None] + within[None, :]).reshape(-1)

time: 391 us -> 313 us (0.80)
  waiting for transfers between devices: 250 us -> 154 us
  starting transfers between devices: 10.5 us -> 30.4 us
    all_gather x1 -> x0, waiting for transfers between devices: 96.8 us -> none  [shards(): lax.all_gather(values[0], 'seq', axis=0, tiled=True)]
    all_to_all x0 -> x1, starting transfers between devices: none -> 20 us  [shards(): lax.all_to_all(jnp.stack(lax.axis_size('seq') * [values[0]], axis=0), spl...]
  transfers between devices with their start and end apart: 4 -> 4, of which waited for: 3 -> 2; matrix products, arithmetic and copies ran while one was open for 13% -> 15% of each run, Pallas kernels for 0% -> 0%
where the time goes in v1:
time: 313 us; the launch traced here: 312 us
  waiting for transfers between devices  154 us (49%)
  other arithmetic  32.8 us (10%)
  starting transfers between devices  30.4 us (10%)
  matrix products  26.8 us (9%)
  local copies, waits for them, and re-layouts  24.5 us (8%)
  blocking collectives  20.8 us (7%)
  between operations  17.7 us (6%)
  loops' own time  4.14 us (1%)
    all_gather x1, waiting for transfers between devices, shards(): lax.all_gather(outgoing, 'seq', axis=0, tiled=True)  129 us
    reduce_scatter x1, waiting for transfers between devices, shards(): lax.psum_scatter(projected.astype(jnp.bfloat16), 'tp', scatter_dimension=...  24.9 us
    all_to_all x1, starting transfers between devices, shards(): lax.all_to_all(jnp.stack(lax.axis_size('seq') * [values[0]], axis=0), spl...  20 us
    psum x1, blocking collectives, shards(): prediction = lax.psum(partial_pred, 'tp')  13.3 us
    ppermute x1, starting transfers between devices, partner_2(): lax.ppermute(shard, axis, [(i, i ^ 1 << distance) for i in range(lax.axis...  10.4 us
    dot_general x12, matrix products, last_dims(): lax.dot_general(left, right, (((1,), (1,)), ((), ())), preferred_element_...  9.89 us
    dot_general x6, matrix products, one_head(): jnp.dot(video_weights.astype(jnp.bfloat16), video_value_part, preferred_e...  8.91 us
    psum x1, blocking collectives, shards(): lax.psum((jnp.sum(widened, axis=1), jnp.sum(widened * widened, axis=1)),...  7.42 us
  transfers between devices with their start and end apart: 4, of which 2 were waited for; matrix products, arithmetic and copies ran while one was open for 15% of the time, Pallas kernels for 0%

profile of v1, /device:TPU:1, one launch (start us, length us, event | category | flops | bytes accessed | tf_op | source)
XLA Modules:
  0.0 311.6 jit_solution(6255174111129203352)
XLA Ops:
  7.2 0.7 all-gather.3.cloned.1.call-update
  7.9 2.2 stack.17
  10.1 20.0 %all-to-all-start = ((bf16[64,40,384]{2,1,0:T(8,128)(2,1)}), bf16[64,40,384]{2,1,0:T(8,128)(2,1)}, u32[]{:S(2)}, u32[]{:S(2)}) async-start(bf16[64,40,384]{2,1,0:T(8,128)(2,1)} %stack.17), calls=%async_computation | async-start | bytes 3932160 | tf_op jit(solution)/shard_map/all_to_all | solution.py:101
  30.5 0.6 fusion.51
  31.3 0.7 fusion.53
  32.0 0.7 fusion.57
  35.9 1.4 fusion.29
  37.3 128.8 %all-gather.3.cloned.1.call-done = bf16[1,2560,384]{2,1,0:T(8,128)(2,1)} async-done(((bf16[1,40,384]{2,1,0:T(8,128)(2,1)}), bf16[1,2560,384]{2,1,0:T(8,128)(2,1)}) %all-gather.3.cloned.1.call-update) | async-done | bytes 1966096 | tf_op jit(solution)/shard_map/all_gather | solution.py:99
  166.1 4.0 %copy.54 = bf16[1,2560,384]{1,2,0:T(8,128)(2,1)} copy(bf16[1,2560,384]{2,1,0:T(8,128)(2,1)} %all-gather.3.cloned.1.call-done) | data formatting | bytes 3932160 | tf_op jit(solution)/shard_map/all_gather | solution.py:99
  170.1 3.9 %convert_element_type.154 = f32[1,2560,384]{1,2,0:T(8,128)} convert(bf16[1,2560,384]{1,2,0:T(8,128)(2,1)} %copy.54) | non-fusion elementwise | flops 983040 | bytes 5898240 | tf_op jit(solution)/shard_map/convert_element_type | solution.py:53
  174.1 2.5 reduce_sum.112
  176.6 5.3 %reshape.429 = f32[2560,6,32,2]{0,3,2,1:T(2,128)} reshape(bf16[1,2560,384]{1,2,0:T(8,128)(2,1)} %copy.54) | data formatting | bytes 5898240 | tf_op jit(solution)/shard_map/reshape | solution.py:53
  181.9 2.8 multiply_reduce_fusion
  185.2 1.8 multiply_multiply_fusion
  187.0 5.2 %subtract_convert_fusion = (bf16[2560,6,32,1]{0,3,2,1:T(2,128)(2,1)S(1)}, bf16[2560,6,32,1]{0,3,2,1:T(2,128)(2,1)S(1)}) fusion(f32[2560,6,32,2]{0,3,2,1:T(2,128)S(1)} %multiply_multiply_fusion, f32[2560,32]{0,1:T(8,128)S(1)} %get-tuple-element.135, f32[2560,32]{0,1:T(8,128)S(1)} %get-tuple-element.134), kind=kLoop, calls=%fused_computation.34 | loop fusion | flops 3932160 | bytes 6553600 | tf_op jit(solution)/shard_map/convert.5
  192.1 5.7 %pad_maximum_fusion = bf16[2560,6,32,2]{0,3,2,1:T(2,128)(2,1)} fusion(bf16[2560,6,32,1]{0,3,2,1:T(2,128)(2,1)S(1)} %get-tuple-element.133, bf16[2560,6,32,1]{0,3,2,1:T(2,128)(2,1)S(1)} %get-tuple-element.132), kind=kLoop, calls=%fused_computation.32 | loop fusion | flops 3932160 | bytes 3932160 | tf_op jit(solution)/shard_map/stack | solution.py:45
  197.9 5.2 %convert_element_type.139 = bf16[2560,384]{0,1:T(8,128)(2,1)} reshape(bf16[2560,6,32,2]{0,3,2,1:T(2,128)(2,1)} %pad_maximum_fusion) | data formatting | bytes 3932160 | tf_op jit(solution)/shard_map/convert_element_type | solution.py:56
  203.1 36.7 %while.11 = (s32[]{:T(128)}, bf16[6,40,64]{2,1,0:T(8,128)(2,1)S(1)}, s32[6]{0:T(128)S(1)}, bf16[40,384]{1,0:T(8,128)(2,1)S(1)}, bf16[2560,384]{0,1:T(8,128)(2,1)...) while((s32[]{:T(128)}, ...), condition=%wide.region_14.15_spmd.clone, body=%wide.region_9.14_spmd.clone.sunk | while | flops 29309844 | bytes 2495583 | solution.py:144
  204.5 1.3 fusion.78
  206.6 1.5 fusion.80
  208.1 1.1 fusion.83
  210.6 1.3 fusion.78
  212.8 1.5 fusion.80
  214.3 1.1 fusion.83
  216.8 1.3 fusion.78
  218.9 1.5 fusion.80
  220.4 1.1 fusion.83
  221.5 0.6 dynamic_slice.78
  222.9 1.3 fusion.78
  225.0 1.5 fusion.80
  226.5 1.1 fusion.83
  227.6 0.6 dynamic_slice.78
  229.0 1.3 fusion.78
  231.1 1.5 fusion.80
  232.6 1.1 fusion.83
  233.7 0.6 dynamic_slice.78
  235.2 1.3 fusion.78
  237.3 1.5 fusion.80
  238.8 1.1 fusion.83
  240.1 1.2 convolution_convert_fusion
  241.3 0.7 iota_compare_fusion.1
  242.0 24.9 %reduce-scatter.2.cloned.1.call-done = bf16[40,768]{1,0:T(8,128)(2,1)} async-done(((bf16[40,3072]{1,0:T(8,128)(2,1)}), bf16[40,768]{1,0:T(8,128)(2,1)}) %reduce-scatter.2.cloned.1.call-update) | async-done | bytes 61456 | tf_op jit(solution)/shard_map/reduce_scatter | solution.py:147
  266.9 0.9 fusion.37
  267.9 7.4 %all-reduce = (f32[40]{0:T(128)S(1)}, f32[40]{0:T(128)S(1)}) all-reduce(f32[40]{0:T(128)S(1)} %get-tuple-element.105, f32[40]{0:T(128)S(1)} %get-tuple-element.104), channel_id=1, replica_groups=mesh['cfg'=2,'seq'=64,'tp'=4] {'tp'}, use_global_device_ids=true, to_apply=%region_19.20 | all-reduce | flops 80 | bytes 640 | tf_op jit(solution)/shard_map/psum | solution.py:153
  275.8 13.3 %psum.23 = f32[40,64]{0,1:T(8,128)S(1)} all-reduce(f32[40,64]{0,1:T(8,128)S(1)} %fusion.33), channel_id=1, replica_groups=mesh['cfg'=2,'seq'=64,'tp'=4] {'tp'}, use_global_device_ids=true, to_apply=%region_20.21 | all-reduce | flops 2560 | bytes 20480 | tf_op jit(solution)/shard_map/psum | solution.py:165
  289.1 10.4 %collective-permute-start = (f32[40,64]{0,1:T(8,128)S(1)}, f32[40,64]{0,1:T(8,128)S(1)}, u32[]{:S(2)}, u32[]{:S(2)}) collective-permute-start(f32[40,64]{0,1:T(8,128)S(1)} %psum.23), channel_id=1, source_target_pairs={{0,256},{256,0},{1,257},{257,1},{2,258},{258,2},{3,259},{259,3},{4... | collective-permute-start | bytes 30728 | tf_op jit(solution)/shard_map/ppermute | solution.py:17
  300.2 1.4 fusion.60
  304.1 0.6 add_select_fusion.4
  (129 shorter events, 12.3 us)
Async XLA Ops:
  7.2 232.9 %copy-start = (bf16[384,3072]{1,0:T(8,128)(2,1)S(1)}, bf16[384,3072]{1,0:T(8,128)(2,1)}, u32[]{:S(2)}) copy-start(bf16[384,3072]{1,0:T(8,128)(2,1)} %param.25) | copy-start | bytes 7077892
  7.2 158.9 %all-gather.3.cloned.1.call-start = ((), (), s32[]{:S(2)}) async-start(), calls=%async_computation.3 | async-start | bytes 1996800 | tf_op jit(solution)/shard_map/all_gather | solution.py:99
  10.1 20.0 %copy-start.7 = (s32[64]{0:T(128)S(1)}, s32[64]{0:T(128)}, u32[]{:S(2)}) copy-start(s32[64]{0:T(128)} %param.32) | copy-start | bytes 772
  10.1 22.6 %copy-start.5 = (bf16[1,40,384]{2,1,0:T(8,128)(2,1)S(1)}, bf16[1,40,384]{2,1,0:T(8,128)(2,1)}, u32[]{:S(2)}) copy-start(bf16[1,40,384]{2,1,0:T(8,128)(2,1)} %param.20) | copy-start | bytes 92164
  10.1 23.3 %copy-start.12 = (f32[64]{0:T(128)S(1)}, f32[64]{0:T(128)}, u32[]{:S(2)}) copy-start(f32[64]{0:T(128)} %param.31) | copy-start | bytes 772
  10.1 24.0 %copy-start.13 = (f32[64]{0:T(128)S(1)}, f32[64]{0:T(128)}, u32[]{:S(2)}) copy-start(f32[64]{0:T(128)} %param.30) | copy-start | bytes 772
  10.1 193.0 %all-to-all-start = ((bf16[64,40,384]{2,1,0:T(8,128)(2,1)}), bf16[64,40,384]{2,1,0:T(8,128)(2,1)}, u32[]{:S(2)}, u32[]{:S(2)}) async-start(bf16[64,40,384]{2,1,0:T(8,128)(2,1)} %stack.17), calls=%async_computation | async-start | bytes 3932160 | tf_op jit(solution)/shard_map/all_to_all | solution.py:101
  30.1 5.1 %copy-start.4 = (bf16[1,226,384]{2,1,0:T(8,128)(2,1)S(1)}, bf16[1,226,384]{2,1,0:T(8,128)(2,1)}, u32[]{:S(2)}) copy-start(bf16[1,226,384]{2,1,0:T(8,128)(2,1)} %param.23) | copy-start | bytes 520708
  30.1 236.8 %reduce-scatter.2.cloned.1.call-start = ((), (), s32[]{:S(2)}) async-start(), calls=%async_computation.2 | async-start | bytes 307200 | tf_op jit(solution)/shard_map/reduce_scatter | solution.py:147
  181.9 3.3 %copy-start.1 = (f32[2560,6,32,2]{0,3,2,1:T(2,128)S(1)}, f32[2560,6,32,2]{0,3,2,1:T(2,128)}, u32[]{:S(2)}) copy-start(f32[2560,6,32,2]{0,3,2,1:T(2,128)} %reshape.429) | copy-start | bytes 11796484
  239.8 2.1 copy-start.11
  239.8 27.1 %copy-start.6 = (bf16[1,40,768]{2,1,0:T(8,128)(2,1)S(1)}, bf16[1,40,768]{2,1,0:T(8,128)(2,1)}, u32[]{:S(2)}) copy-start(bf16[1,40,768]{2,1,0:T(8,128)(2,1)} %param.19) | copy-start | bytes 184324
  239.9 27.0 %copy-start.9 = (f32[768]{0:T(1024)S(1)}, f32[768]{0:T(1024)}, u32[]{:S(2)}) copy-start(f32[768]{0:T(1024)} %param.26) | copy-start | bytes 9220
  239.9 35.5 %copy-start.3 = (f32[768,64]{0,1:T(8,128)S(1)}, f32[768,64]{0,1:T(8,128)}, u32[]{:S(2)}) copy-start(f32[768,64]{0,1:T(8,128)} %param.29) | copy-start | bytes 589828
  239.9 35.5 %copy-start.8 = (f32[768]{0:T(1024)S(1)}, f32[768]{0:T(1024)}, u32[]{:S(2)}) copy-start(f32[768]{0:T(1024)} %param.27) | copy-start | bytes 9220
  239.9 64.2 %copy-start.10 = (f32[40,8]{0,1:T(8,128)S(1)}, f32[40,8]{0,1:T(8,128)}, u32[]{:S(2)}) copy-start(f32[40,8]{0,1:T(8,128)} %param.33) | copy-start | bytes 3844
  267.8 36.9 %copy-start.2 = (bf16[40,768]{1,0:T(8,128)(2,1)}, bf16[40,768]{1,0:T(8,128)(2,1)S(1)}, u32[]{:S(2)}) copy-start(bf16[40,768]{1,0:T(8,128)(2,1)S(1)} %fusion.37) | copy-start | bytes 184324
  289.1 15.0 %collective-permute-start = (f32[40,64]{0,1:T(8,128)S(1)}, f32[40,64]{0,1:T(8,128)S(1)}, u32[]{:S(2)}, u32[]{:S(2)}) collective-permute-start(f32[40,64]{0,1:T(8,128)S(1)} %psum.23), channel_id=1, source_target_pairs={{0,256},{256,0},{1,257},{257,1},{2,258},{258,2},{3,259},{259,3},{4... | collective-permute-start | bytes 30728 | tf_op jit(solution)/shard_map/ppermute | solution.py:17
Sparse Core Ops, SparseCore 0:
  12.3 153.7 all-gather.2
  241.4 25.4 reduce-scatter.1
